TPU v7x, 32 devices: a whole 2x2x4 slice. The times are simulated.
32 devices in a mesh: enc: 4 (over z), dp: 8 (over y, x, core).
Axes of the slice: x: 2, y: 2, z: 4, core: 2. Of those that a mesh axis runs over, the one named last changes fastest.
Arguments:
- text: bfloat16 [16384, 768], P(('enc', 'dp')), may hold values from -6 to 6
- region_feats: bfloat16 [13312, 2048], P(('enc', 'dp')), may hold values from -6 to 6
- boxes: bfloat16 [4, 13312], P(None, ('enc', 'dp')), may hold values from 0 to 1
- caption_count: int32 [128], P(('enc', 'dp')), may hold values from 8 to 128, as said below
- region_count: int32 [128], P(('enc', 'dp')), may hold values from 36 to 100, as said below
- region_offset: int32 [32], P(('enc', 'dp')), may hold values from 0 to 31
- w_img: bfloat16 [2048, 768], P(('enc', 'dp')), may hold values from -0.125 to 0.125
- w_box: bfloat16 [4, 768], replicated, may hold values from -3 to 3
- b_img: float32 [768], replicated, may hold values from -3 to 3
- g_reg: float32 [768], replicated, may hold values from 0.25 to 1.75
- beta_reg: float32 [768], replicated, may hold values from -1.75 to 1.75
- w_query: bfloat16 [768, 768], P(('enc', 'dp')), may hold values from -0.21875 to 0.21875
- b_query: float32 [768], replicated, may hold values from -1.75 to 1.75
- w_key: bfloat16 [768, 768], P(('enc', 'dp')), may hold values from -0.21875 to 0.21875
- w_value: bfloat16 [768, 768], P(('enc', 'dp')), may hold values from -0.21875 to 0.21875
- b_value: float32 [768], replicated, may hold values from -1.75 to 1.75
- w_out: bfloat16 [768, 768], P(('enc', 'dp')), may hold values from -1.75 to 1.75
- b_out: float32 [768], replicated, may hold values from -1.75 to 1.75
- g_one: float32 [768], replicated, may hold values from 0.25 to 1.75
- beta_one: float32 [768], replicated, may hold values from -1.75 to 1.75
- w_up: bfloat16 [768, 3072], P(('enc', 'dp')), may hold values from -0.21875 to 0.21875
- b_up: float32 [3072], replicated, may hold values from -1.75 to 1.75
- w_down: bfloat16 [3072, 768], P(('enc', 'dp')), may hold values from -0.109375 to 0.109375
- b_down: float32 [768], replicated, may hold values from -1.75 to 1.75
- g_two: float32 [768], replicated, may hold values from 0.25 to 1.75
- beta_two: float32 [768], replicated, may hold values from -1.75 to 1.75
- cotangent: bfloat16 [32768, 768], P(('enc', 'dp'))
Outputs:
- output: bfloat16 [32768, 768], P(('enc', 'dp'))
- grad_text: bfloat16 [16384, 768], P(('enc', 'dp'))
- grad_feats: bfloat16 [13312, 2048], P(('enc', 'dp'))
- grad_boxes: bfloat16 [4, 13312], P(None, ('enc', 'dp'))
- grad_w_img: float32 [2048, 768], replicated
- grad_w_box: float32 [4, 768], replicated
- grad_b_img: float32 [768], replicated
- grad_g_reg: float32 [768], replicated
- grad_beta_reg: float32 [768], replicated
- grad_w_query: float32 [768, 768], replicated
- grad_b_query: float32 [768], replicated
- grad_w_key: float32 [768, 768], replicated
- grad_w_value: float32 [768, 768], replicated
- grad_b_value: float32 [768], replicated
- grad_w_out: float32 [768, 768], replicated
- grad_b_out: float32 [768], replicated
- grad_g_one: float32 [768], replicated
- grad_beta_one: float32 [768], replicated
- grad_w_up: float32 [768, 3072], replicated
- grad_b_up: float32 [3072], replicated
- grad_w_down: float32 [3072, 768], replicated
- grad_b_down: float32 [768], replicated
- grad_g_two: float32 [768], replicated
- grad_beta_two: float32 [768], replicated
Inputs may be any that keep to these rules, and one draw needn't show every extreme that they name: `caption_count`: some sequence has exactly 128 caption tokens. `region_count`: in every draw some holder's 4 sequences all have 100 regions.
All inputs are finite; a program needn't handle non-finite values.
Results may differ from a plain program's by a relative error of at most 0.018.
Values may be sent and summed in bfloat16 or wider, within the bound.
No kernel may reach another device: no remote copies, remote signals or barrier semaphores. Data moves between devices by JAX's collectives and lax.ppermute only.
A program may use at most 192 MiB of HBM per device.

v0:
```python
import jax
import jax.numpy as jnp
from jax import lax
from jax.sharding import PartitionSpec as P

HEADS = 12
epsilon = 1e-05


def normalize(values, gain_vec, shift_vec):
    centered = values - jnp.mean(values, -1, keepdims=True)
    inverse = lax.rsqrt(jnp.mean(centered * centered, -1, keepdims=True) + epsilon)
    normed = centered * inverse
    return (normed * gain_vec + shift_vec, normed, inverse)


def normalize_back(upstream, normed, inverse, gain_vec):
    weighted = upstream * gain_vec
    result = inverse * (
        weighted
        - jnp.mean(weighted, -1, keepdims=True)
        - normed * jnp.mean(weighted * normed, -1, keepdims=True)
    )
    return (result, jnp.sum(upstream * normed, 0), jnp.sum(upstream, 0))


def exact_gelu(values):
    return jax.nn.gelu(values, approximate=False)


def outer_sum(row_data, row_grad):
    return jnp.einsum("ra,rb->ab", row_data, row_grad, preferred_element_type=jnp.float32)


def back_product(row_grad, weight):
    return jnp.einsum("rb,ab->ra", row_grad, weight, preferred_element_type=jnp.float32)


def column_sum(row_grad):
    return jnp.sum(row_grad.astype(jnp.float32), 0)


def body(
    text,
    region_feats,
    boxes,
    caption_count,
    region_count,
    region_offset,
    w_img,
    w_box,
    b_img,
    g_reg,
    beta_reg,
    w_query,
    b_query,
    w_key,
    w_value,
    b_value,
    w_out,
    b_out,
    g_one,
    beta_one,
    w_up,
    b_up,
    w_down,
    b_down,
    g_two,
    beta_two,
    cotangent,
):
    img_full, query_full, key_full, value_full, out_full, up_full, down_full = (
        lax.all_gather(w_img, ("enc", "dp"), axis=0, tiled=True),
        lax.all_gather(w_query, ("enc", "dp"), axis=0, tiled=True),
        lax.all_gather(w_key, ("enc", "dp"), axis=0, tiled=True),
        lax.all_gather(w_value, ("enc", "dp"), axis=0, tiled=True),
        lax.all_gather(w_out, ("enc", "dp"), axis=0, tiled=True),
        lax.all_gather(w_up, ("enc", "dp"), axis=0, tiled=True),
        lax.all_gather(w_down, ("enc", "dp"), axis=0, tiled=True),
    )
    device_count = lax.axis_size(("enc", "dp"))
    seq_count = caption_count.shape[0]
    model_width = text.shape[1]
    text_len = text.shape[0] // seq_count
    seq_len = cotangent.shape[0] // seq_count
    region_len = seq_len - text_len
    sent_rows = region_feats.shape[0]
    per_peer = sent_rows // device_count
    head_dim = model_width // HEADS
    score_scale = head_dim ** (-0.5)
    pre_norm = (
        jnp.dot(region_feats, img_full, preferred_element_type=jnp.float32)
        + jnp.einsum("cr,cd->rd", boxes, w_box, preferred_element_type=jnp.float32)
        + b_img
    )
    encoded, enc_normed, enc_inverse = normalize(pre_norm, g_reg, beta_reg)
    received = lax.all_to_all(
        encoded.astype(jnp.bfloat16), ("enc", "dp"), split_axis=0, concat_axis=0, tiled=True
    )
    position = jnp.arange(sent_rows, dtype=jnp.int32)
    arrival = (
        position % per_peer * device_count
        + (position // per_peer - region_offset[0]) % device_count
    )
    starts = jnp.cumsum(region_count) - region_count
    slot_total = seq_count * region_len
    slot_pos = jnp.arange(slot_total, dtype=jnp.int32) % region_len
    wanted = jnp.repeat(starts, region_len, total_repeat_length=slot_total) + slot_pos
    slot_live = slot_pos < jnp.repeat(region_count, region_len, total_repeat_length=slot_total)
    placement = ((wanted[:, None] == arrival[None, :]) & slot_live[:, None]).astype(jnp.bfloat16)
    regions = jnp.dot(placement, received, preferred_element_type=jnp.float32).astype(jnp.bfloat16)
    hidden_in = jnp.concatenate(
        [
            text.reshape(seq_count, text_len, model_width),
            regions.reshape(seq_count, region_len, model_width),
        ],
        1,
    ).reshape(seq_count * seq_len, model_width)
    key_live = jnp.concatenate(
        [
            jnp.arange(text_len)[None, :] < caption_count[:, None],
            jnp.arange(region_len)[None, :] < region_count[:, None],
        ],
        1,
    )
    row_live = key_live.reshape(-1, 1).astype(jnp.float32)

    def heads_view(tensor):
        return tensor.reshape(seq_count, seq_len, HEADS, head_dim)

    query_heads = heads_view(
        (jnp.dot(hidden_in, query_full, preferred_element_type=jnp.float32) + b_query).astype(
            jnp.bfloat16
        )
    )
    key_heads = heads_view(
        jnp.dot(hidden_in, key_full, preferred_element_type=jnp.float32).astype(jnp.bfloat16)
    )
    value_heads = heads_view(
        (jnp.dot(hidden_in, value_full, preferred_element_type=jnp.float32) + b_value).astype(
            jnp.bfloat16
        )
    )
    scores = (
        jnp.einsum("sqhd,skhd->shqk", query_heads, key_heads, preferred_element_type=jnp.float32)
        * score_scale
    )
    scores = jnp.where(key_live[:, None, None, :], scores, -1e30)
    row_max = jnp.max(scores, -1, keepdims=True)
    exp_scores = jnp.exp(scores - row_max)
    attn_probs = exp_scores / jnp.sum(exp_scores, -1, keepdims=True)
    probs_low = attn_probs.astype(jnp.bfloat16)
    context = (
        jnp.einsum("shqk,skhd->sqhd", probs_low, value_heads, preferred_element_type=jnp.float32)
        .reshape(-1, model_width)
        .astype(jnp.bfloat16)
    )
    mixed = (
        hidden_in.astype(jnp.float32)
        + jnp.dot(context, out_full, preferred_element_type=jnp.float32)
        + b_out
    )
    normed_one, one_normed, one_inverse = normalize(mixed, g_one, beta_one)
    normed_one = normed_one.astype(jnp.bfloat16)
    gate_in = jnp.dot(normed_one, up_full, preferred_element_type=jnp.float32) + b_up
    activated = exact_gelu(gate_in).astype(jnp.bfloat16)
    second_in = (
        normed_one.astype(jnp.float32)
        + jnp.dot(activated, down_full, preferred_element_type=jnp.float32)
        + b_down
    )
    normed_two, two_normed, two_inverse = normalize(second_in, g_two, beta_two)
    output = (normed_two * row_live).astype(jnp.bfloat16)
    grad_second = cotangent.astype(jnp.float32) * row_live
    grad_second_in, grad_g_two, grad_beta_two = normalize_back(
        grad_second, two_normed, two_inverse, g_two
    )
    grad_down_out = grad_second_in.astype(jnp.bfloat16)
    grad_w_down = outer_sum(activated, grad_down_out)
    grad_b_down = column_sum(grad_down_out)
    grad_activated = back_product(grad_down_out, down_full)
    gelu_pull = jax.vjp(exact_gelu, gate_in)[1]
    grad_gate = gelu_pull(grad_activated)[0].astype(jnp.bfloat16)
    grad_w_up = outer_sum(normed_one, grad_gate)
    grad_b_up = column_sum(grad_gate)
    grad_first = back_product(grad_gate, up_full) + grad_second_in
    grad_mixed, grad_g_one, grad_beta_one = normalize_back(
        grad_first, one_normed, one_inverse, g_one
    )
    grad_attn = grad_mixed.astype(jnp.bfloat16)
    grad_w_out = outer_sum(context, grad_attn)
    grad_b_out = column_sum(grad_attn)
    grad_context = heads_view(back_product(grad_attn, out_full).astype(jnp.bfloat16))
    grad_probs = jnp.einsum(
        "sqhd,skhd->shqk", grad_context, value_heads, preferred_element_type=jnp.float32
    )
    grad_values = (
        jnp.einsum("shqk,sqhd->skhd", probs_low, grad_context, preferred_element_type=jnp.float32)
        .reshape(-1, model_width)
        .astype(jnp.bfloat16)
    )
    grad_scores = (
        attn_probs * (grad_probs - jnp.sum(attn_probs * grad_probs, -1, keepdims=True))
    ).astype(jnp.bfloat16)
    grad_query = (
        (
            jnp.einsum(
                "shqk,skhd->sqhd", grad_scores, key_heads, preferred_element_type=jnp.float32
            )
            * score_scale
        )
        .reshape(-1, model_width)
        .astype(jnp.bfloat16)
    )
    grad_keys = (
        (
            jnp.einsum(
                "shqk,sqhd->skhd", grad_scores, query_heads, preferred_element_type=jnp.float32
            )
            * score_scale
        )
        .reshape(-1, model_width)
        .astype(jnp.bfloat16)
    )
    grad_w_query = outer_sum(hidden_in, grad_query)
    grad_b_query = column_sum(grad_query)
    grad_w_key = outer_sum(hidden_in, grad_keys)
    grad_w_value = outer_sum(hidden_in, grad_values)
    grad_b_value = column_sum(grad_values)
    grad_hidden = (
        grad_mixed
        + back_product(grad_query, query_full)
        + back_product(grad_keys, key_full)
        + back_product(grad_values, value_full)
    )
    grad_hidden = grad_hidden.reshape(seq_count, seq_len, model_width)
    grad_text = grad_hidden[:, :text_len].reshape(-1, model_width).astype(jnp.bfloat16)
    grad_slots = grad_hidden[:, text_len:].reshape(-1, model_width).astype(jnp.bfloat16)
    grad_sent = jnp.einsum(
        "tn,td->nd", placement, grad_slots, preferred_element_type=jnp.float32
    ).astype(jnp.bfloat16)
    grad_encoded = lax.all_to_all(
        grad_sent, ("enc", "dp"), split_axis=0, concat_axis=0, tiled=True
    ).astype(jnp.float32)
    grad_pre, grad_g_reg, grad_beta_reg = normalize_back(
        grad_encoded, enc_normed, enc_inverse, g_reg
    )
    grad_pre = grad_pre.astype(jnp.bfloat16)
    grad_w_img = outer_sum(region_feats, grad_pre)
    grad_w_box = jnp.einsum("cr,rd->cd", boxes, grad_pre, preferred_element_type=jnp.float32)
    grad_b_img = column_sum(grad_pre)
    grad_feats = back_product(grad_pre, img_full).astype(jnp.bfloat16)
    grad_boxes = jnp.einsum(
        "cd,rd->cr", w_box, grad_pre, preferred_element_type=jnp.float32
    ).astype(jnp.bfloat16)
    (
        grad_w_img,
        grad_w_box,
        grad_b_img,
        grad_g_reg,
        grad_beta_reg,
        grad_w_query,
        grad_b_query,
        grad_w_key,
        grad_w_value,
        grad_b_value,
        grad_w_out,
        grad_b_out,
        grad_g_one,
        grad_beta_one,
        grad_w_up,
        grad_b_up,
        grad_w_down,
        grad_b_down,
        grad_g_two,
        grad_beta_two,
    ) = lax.psum(
        (
            grad_w_img,
            grad_w_box,
            grad_b_img,
            grad_g_reg,
            grad_beta_reg,
            grad_w_query,
            grad_b_query,
            grad_w_key,
            grad_w_value,
            grad_b_value,
            grad_w_out,
            grad_b_out,
            grad_g_one,
            grad_beta_one,
            grad_w_up,
            grad_b_up,
            grad_w_down,
            grad_b_down,
            grad_g_two,
            grad_beta_two,
        ),
        ("enc", "dp"),
    )
    return (
        output,
        grad_text,
        grad_feats,
        grad_boxes,
        grad_w_img,
        grad_w_box,
        grad_b_img,
        grad_g_reg,
        grad_beta_reg,
        grad_w_query,
        grad_b_query,
        grad_w_key,
        grad_w_value,
        grad_b_value,
        grad_w_out,
        grad_b_out,
        grad_g_one,
        grad_beta_one,
        grad_w_up,
        grad_b_up,
        grad_w_down,
        grad_b_down,
        grad_g_two,
        grad_beta_two,
    )


def solution(mesh):
    return jax.shard_map(
        body,
        mesh=mesh,
        in_specs=(
            P(("enc", "dp"), None),
            P(("enc", "dp"), None),
            P(None, ("enc", "dp")),
            P(("enc", "dp")),
            P(("enc", "dp")),
            P(("enc", "dp")),
            P(("enc", "dp"), None),
            P(),
            P(),
            P(),
            P(),
            P(("enc", "dp"), None),
            P(),
            P(("enc", "dp"), None),
            P(("enc", "dp"), None),
            P(),
            P(("enc", "dp"), None),
            P(),
            P(),
            P(),
            P(("enc", "dp"), None),
            P(),
            P(("enc", "dp"), None),
            P(),
            P(),
            P(),
            P(("enc", "dp"), None),
        ),
        out_specs=(
            P(("enc", "dp"), None),
            P(("enc", "dp"), None),
            P(("enc", "dp"), None),
            P(None, ("enc", "dp")),
            P(),
            P(),
            P(),
            P(),
            P(),
            P(),
            P(),
            P(),
            P(),
            P(),
            P(),
            P(),
            P(),
            P(),
            P(),
            P(),
            P(),
            P(),
            P(),
            P(),
        ),
        check_vma=False,
    )
```

profile of v0, /device:TPU:0, one launch (start us, length us, event | category | flops | bytes accessed | tf_op | source)
XLA Modules:
  0.0 1141.4 jit_solution(5793821062588575223)
XLA Ops:
  11.2 61.4 %all-gather.8.cloned.1.call-done = bf16[2048,768]{1,0:T(8,128)(2,1)} async-done(((bf16[64,768]{1,0:T(8,128)(2,1)}), bf16[2048,768]{1,0:T(8,128)(2,1)}) %all-gather.8.cloned.1.call-update) | async-done | bytes 3145744 | tf_op jit(solution)/shard_map/all_gather | solution.py:73
  72.6 3.4 fusion.82
  79.5 3.4 all-to-all-start
  85.8 2.6 select_compare_fusion
  89.0 2.6 select_add_fusion
  91.7 12.7 %all-to-all-done = bf16[32,13,768]{2,1,0:T(8,128)(2,1)S(1)} async-done(((bf16[32,13,768]{2,1,0:T(8,128)(2,1)}), bf16[32,13,768]{2,1,0:T(8,128)(2,1)S(1)}, u32[]{:S(2)}, u32[]{:S(2)}) %all-to-all-start) | async-done | bytes 639008 | tf_op jit(solution)/shard_map/all_to_all | solution.py:97
  106.5 24.1 %all-gather.14.cloned.1.call-done = bf16[768,768]{1,0:T(8,128)(2,1)} async-done(((bf16[24,768]{1,0:T(8,128)(2,1)}), bf16[768,768]{1,0:T(8,128)(2,1)}) %all-gather.14.cloned.1.call-update) | async-done | bytes 1179664 | tf_op jit(solution)/shard_map/all_gather | solution.py:75
  130.7 3.8 convolution_convert_fusion.2
  134.5 1.7 copy.66
  136.2 2.4 reshape.314
  138.6 48.0 %all-gather.12.cloned.1.call-done = bf16[768,768]{1,0:T(8,128)(2,1)} async-done(((bf16[24,768]{1,0:T(8,128)(2,1)}), bf16[768,768]{1,0:T(8,128)(2,1)}) %all-gather.12.cloned.1.call-update) | async-done | bytes 1179664 | tf_op jit(solution)/shard_map/all_gather | solution.py:74
  186.6 3.1 add_convert_fusion.3
  189.7 1.6 copy.65
  191.4 2.9 reshape.313
  194.3 48.1 %all-gather.10.cloned.1.call-done = bf16[768,768]{1,0:T(8,128)(2,1)} async-done(((bf16[24,768]{1,0:T(8,128)(2,1)}), bf16[768,768]{1,0:T(8,128)(2,1)}) %all-gather.10.cloned.1.call-update) | async-done | bytes 1179664 | tf_op jit(solution)/shard_map/all_gather | solution.py:76
  242.3 4.3 add_convert_fusion.4
  246.6 2.6 copy.64
  249.2 3.9 reshape.312
  253.0 7.8 fusion.39
  260.8 12.9 %fusion.78 = (f32[4,12,256]{2,1,0:T(8,128)S(1)}, f32[4,12,256,256]{2,3,1,0:T(8,128)S(1)}) fusion(f32[4,12,256,256]{2,3,1,0:T(8,128)} %fusion.39, pred[4,256]{1,0:T(4,128)(4,1)S(1)} %get-tuple-element.137), kind=kOutput, calls=%fused_computation.163 | output fusion | flops 18874624 | bytes 25216000 | tf_op jit(solution)/shard_map/sub | solution.py:150
  274.9 3.4 copy-done.8
  279.7 1.5 copy.89
  281.2 16.9 %all-gather.16.cloned.1.call-done = bf16[768,768]{1,0:T(8,128)(2,1)} async-done(((bf16[24,768]{1,0:T(8,128)(2,1)}), bf16[768,768]{1,0:T(8,128)(2,1)}) %all-gather.16.cloned.1.call-update) | async-done | bytes 1179664 | tf_op jit(solution)/shard_map/all_gather | solution.py:77
  298.1 3.4 fusion.79
  301.6 1.6 copy-done.3
  303.8 59.7 %all-gather.18.cloned.1.call-done = bf16[768,3072]{1,0:T(8,128)(2,1)} async-done(((bf16[24,3072]{1,0:T(8,128)(2,1)}), bf16[768,3072]{1,0:T(8,128)(2,1)}) %all-gather.18.cloned.1.call-update) | async-done | bytes 4718608 | tf_op jit(solution)/shard_map/all_gather | solution.py:78
  363.4 38.1 %multiply_convert_fusion.1 = (bf16[1024,3072]{1,0:T(8,128)(2,1)}, f32[1024,3072]{1,0:T(8,128)}, f32[1024,3072]{1,0:T(8,128)}) fusion(f32[3072]{0:T(1024)S(1)} %copy-done.60, bf16[768,3072]{1,0:T(8,128)(2,1)} %all-gather.18.cloned.1.call-done, f32[1024,768]{1,0:T(8,128)} %copy-done.3, f32[768]{0:T(1024)S(1)} %copy-done.34, f32[768]{0:T(1024)S(1)} %copy-done.29, ...), kind=kOutput, calls=%fused_computation.7 | convolution fusion | flops 5043388416 | bytes 39348224 | tf_op jit(solution)/shard_map/dot_general | solution.py:165
  401.5 27.3 %all-gather.20.cloned.1.call-done = bf16[3072,768]{1,0:T(8,128)(2,1)} async-done(((bf16[96,768]{1,0:T(8,128)(2,1)}), bf16[3072,768]{1,0:T(8,128)(2,1)}) %all-gather.20.cloned.1.call-update) | async-done | bytes 4718608 | tf_op jit(solution)/shard_map/all_gather | solution.py:79
  428.8 9.3 fusion.80
  439.6 2.4 multiply_reduce_fusion.1
  442.0 3.7 convert_reduce_fusion.1
  445.8 7.8 fusion.68
  453.6 18.8 %convert_reduce_fusion = (f32[3072]{0:T(1024)S(1)}, bf16[1024,3072]{1,0:T(8,128)(2,1)}) fusion(f32[1024,3072]{1,0:T(8,128)} %get-tuple-element.132, bf16[3072,768]{1,0:T(8,128)(2,1)} %all-gather.20.cloned.1.call-done, f32[1024,768]{1,0:T(8,128)} %copy-done.15, f32[1024,3072]{1,0:T(8,128)} %get-tuple-element.152, f32[3072]{0:T(1024)S(1)} %copy-done.60), kind=kOutput, calls=%fused_computation.3 | convolution fusion | flops 4886098944 | bytes 39346176 | tf_op jit(solution)/shard_map/rb,ab->ra/dot_general | solution.py:36
  472.4 10.1 multiply_reduce_fusion.2
  483.9 2.8 fusion.65
  486.7 2.6 convolution_convert_fusion.1
  489.3 1.7 copy.72
  491.1 2.4 reshape.315
  493.4 7.3 convert_reduce_fusion.3
  500.8 8.9 multiply_reduce_fusion
  509.7 6.9 multiply_convert_fusion
  516.7 2.0 fusion.31
  521.6 2.9 fusion.87
  527.6 2.9 fusion.85
  530.5 2.9 fusion.86
  533.4 1.7 fusion.83
  535.1 1.5 fusion.84
  537.3 1.6 add_convert_fusion.1
  541.7 3.5 all-to-all-start.1
  545.3 11.0 fusion.81
  556.3 9.5 all-to-all-done.1
  565.9 1.5 convert_reduce_fusion.6
  567.5 2.3 reshape.319
  569.8 1.9 multiply_reduce_fusion.9
  573.0 4.5 convolution_bitcast_fusion
  578.8 43.5 %all-reduce = (f32[4,768]{1,0:T(4,128)}, f32[768]{0:T(1024)}, f32[768]{0:T(1024)}, f32[768]{0:T(1024)}, f32[768]{0:T(1024)}, /*index=5*/f32[768]{0:T(1024)}, f32...) all-reduce(f32[4,768]{1,0:T(4,128)S(1)} %convolution_bitcast_fusion, ...), channel_id=1, replica_groups=mesh['enc'=4,'dp'=8] {'enc','dp'}, use_global_device_ids=true, to_apply=%region_17.19 | all-reduce | flops 14592 | bytes 116736 | tf_op jit(solution)/shard_map/psum | solution.py:277
  623.3 4.9 convolution_convert_fusion
  628.2 476.7 %all-reduce.4.cloned.1.call-done = (f32[2048,768]{0,1:T(8,128)}, f32[768,768]{1,0:T(8,128)}, f32[768,768]{1,0:T(8,128)}, f32[768,768]{1,0:T(8,128)}, f32[768,768...) async-done(((f32[2048,768]{0,1:T(8,128)}, f32[768,768]{1,0:T(8,128)}, f32[768,768]{1,0:T(8,128)}, f32[768,768]{1,0:T(8,128)}, f32[768,768]{1,0:T(8,128)}, ...) | async-done | bytes 34603024 | tf_op jit(solution)/shard_map/psum | solution.py:277
  1104.9 6.6 copy.84
  1111.4 3.4 copy.126
  1114.8 1.4 copy.127
  1117.3 1.4 copy.128
  1121.2 9.3 copy.130
  1130.6 3.7 copy.131
  (212 shorter events, 35.1 us)
Async XLA Ops:
  7.2 65.4 %copy-start = (bf16[416,2048]{1,0:T(8,128)(2,1)S(1)}, bf16[416,2048]{1,0:T(8,128)(2,1)}, u32[]{:S(2)}) copy-start(bf16[416,2048]{1,0:T(8,128)(2,1)} %param.34) | copy-start | bytes 5111812
  7.2 65.4 %all-gather.8.cloned.1.call-start = ((), (), s32[]{:S(2)}) async-start(), calls=%async_computation.2 | async-start | bytes 3244032 | tf_op jit(solution)/shard_map/all_gather | solution.py:73
  7.9 122.7 %all-gather.14.cloned.1.call-start = ((), (), s32[]{:S(2)}) async-start(), calls=%async_computation.5 | async-start | bytes 1216512 | tf_op jit(solution)/shard_map/all_gather | solution.py:75
  8.7 177.9 %all-gather.12.cloned.1.call-start = ((), (), s32[]{:S(2)}) async-start(), calls=%async_computation.4 | async-start | bytes 1216512 | tf_op jit(solution)/shard_map/all_gather | solution.py:74
  9.4 232.9 %all-gather.10.cloned.1.call-start = ((), (), s32[]{:S(2)}) async-start(), calls=%async_computation.3 | async-start | bytes 1216512 | tf_op jit(solution)/shard_map/all_gather | solution.py:76
  10.0 288.1 %all-gather.16.cloned.1.call-start = ((), (), s32[]{:S(2)}) async-start(), calls=%async_computation.6 | async-start | bytes 1216512 | tf_op jit(solution)/shard_map/all_gather | solution.py:77
  10.6 352.9 %all-gather.18.cloned.1.call-start = ((), (), s32[]{:S(2)}) async-start(), calls=%async_computation.7 | async-start | bytes 4866048 | tf_op jit(solution)/shard_map/all_gather | solution.py:78
  11.2 64.8 %copy-start.38 = (bf16[4,768]{1,0:T(4,128)(2,1)S(1)}, bf16[4,768]{1,0:T(4,128)(2,1)}, u32[]{:S(2)}) copy-start(bf16[4,768]{1,0:T(4,128)(2,1)} %param.40) | copy-start | bytes 18436
  11.2 64.8 %copy-start.41 = (bf16[4,416]{1,0:T(4,128)(2,1)S(1)}, bf16[4,416]{1,0:T(4,128)(2,1)}, u32[]{:S(2)}) copy-start(bf16[4,416]{1,0:T(4,128)(2,1)} %param.35) | copy-start | bytes 9988
  11.2 64.8 %copy-start.47 = (f32[768]{0:T(1024)S(1)}, f32[768]{0:T(1024)}, u32[]{:S(2)}) copy-start(f32[768]{0:T(1024)} %param.41) | copy-start | bytes 9220
  76.0 2.1 copy-start.30
  76.0 2.1 copy-start.48
  76.5 7.8 copy-start.46
  76.5 7.8 copy-start.56
  79.5 24.9 %all-to-all-start = ((bf16[32,13,768]{2,1,0:T(8,128)(2,1)}), bf16[32,13,768]{2,1,0:T(8,128)(2,1)S(1)}, u32[]{:S(2)}, u32[]{:S(2)}) async-start(bf16[32,13,768]{2,1,0:T(8,128)(2,1)} %all_to_all.14), calls=%async_computation | async-start | bytes 1572864 | tf_op jit(solution)/shard_map/all_to_all | solution.py:97
  82.9 345.9 %all-gather.20.cloned.1.call-start = ((), (), s32[]{:S(2)}) async-start(), calls=%async_computation.8 | async-start | bytes 4866048 | tf_op jit(solution)/shard_map/all_gather | solution.py:79
  88.4 16.9 %copy-start.54 = (pred[512]{0:T(512)(128)(4,1)}, pred[512]{0:T(512)(128)(4,1)S(1)}, u32[]{:S(2)}) copy-start(pred[512]{0:T(512)(128)(4,1)S(1)} %select_compare_fusion) | copy-start | bytes 1540
  88.4 16.8 %copy-start.50 = (s32[416]{0:T(512)}, s32[416]{0:T(512)S(1)}, u32[]{:S(2)}) copy-start(s32[416]{0:T(512)S(1)} %fusion.52) | copy-start | bytes 4996
  91.6 13.6 %copy-start.52 = (s32[512]{0:T(512)}, s32[512]{0:T(512)S(1)}, u32[]{:S(2)}) copy-start(s32[512]{0:T(512)S(1)} %select_add_fusion) | copy-start | bytes 6148
  106.5 24.1 %copy-start.19 = (bf16[4,256,768]{2,1,0:T(8,128)(2,1)}, bf16[4,256,768]{2,1,0:T(8,128)(2,1)S(1)}, u32[]{:S(2)}) copy-start(bf16[4,256,768]{2,1,0:T(8,128)(2,1)S(1)} %pad_maximum_fusion) | copy-start | bytes 4718596
  134.5 52.1 %copy-start.61 = (f32[768]{0:T(1024)S(1)}, f32[768]{0:T(1024)}, u32[]{:S(2)}) copy-start(f32[768]{0:T(1024)} %param.45) | copy-start | bytes 9220
  189.7 52.6 %copy-start.62 = (f32[768]{0:T(1024)S(1)}, f32[768]{0:T(1024)}, u32[]{:S(2)}) copy-start(f32[768]{0:T(1024)} %param.48) | copy-start | bytes 9220
  194.2 58.8 %copy-start.5 = (bf16[4,256,12,64]{1,0,3,2:T(4,128)(2,1)}, bf16[4,256,12,64]{1,0,3,2:T(4,128)(2,1)S(1)}, u32[]{:S(2)}) copy-start(bf16[4,256,12,64]{1,0,3,2:T(4,128)(2,1)S(1)} %reshape.313) | copy-start | bytes 4718596
  260.8 12.9 %copy-start.22 = (bf16[4,256,12,64]{1,0,3,2:T(4,128)(2,1)S(1)}, bf16[4,256,12,64]{1,0,3,2:T(4,128)(2,1)}, u32[]{:S(2)}) copy-start(bf16[4,256,12,64]{1,0,3,2:T(4,128)(2,1)} %reshape.312) | copy-start | bytes 4718596
  273.7 4.5 copy-start.8
  273.7 4.8 copy-start.27
  278.5 19.6 %copy-start.20 = (bf16[4,256,768]{2,1,0:T(8,128)(2,1)S(1)}, bf16[4,256,768]{2,1,0:T(8,128)(2,1)}, u32[]{:S(2)}) copy-start(bf16[4,256,768]{2,1,0:T(8,128)(2,1)} %copy-done.19) | copy-start | bytes 4718596
  278.5 19.6 %copy-start.63 = (f32[768]{0:T(1024)S(1)}, f32[768]{0:T(1024)}, u32[]{:S(2)}) copy-start(f32[768]{0:T(1024)} %param.50) | copy-start | bytes 9220
  301.5 61.9 %copy-start.29 = (f32[768]{0:T(1024)S(1)}, f32[768]{0:T(1024)}, u32[]{:S(2)}) copy-start(f32[768]{0:T(1024)} %param.51) | copy-start | bytes 9220
  301.5 61.9 %copy-start.34 = (f32[768]{0:T(1024)S(1)}, f32[768]{0:T(1024)}, u32[]{:S(2)}) copy-start(f32[768]{0:T(1024)} %param.52) | copy-start | bytes 9220
  301.5 61.9 %copy-start.60 = (f32[3072]{0:T(1024)S(1)}, f32[3072]{0:T(1024)}, u32[]{:S(2)}) copy-start(f32[3072]{0:T(1024)} %param.54) | copy-start | bytes 36868
  303.7 125.1 %copy-start.64 = (f32[768]{0:T(1024)S(1)}, f32[768]{0:T(1024)}, u32[]{:S(2)}) copy-start(f32[768]{0:T(1024)} %param.56) | copy-start | bytes 9220
  438.7 3.3 copy-start.49
  439.6 6.2 slice-start.6
  442.0 3.7 slice-start.7
  445.8 7.8 copy-start.15
  453.6 18.8 %copy-start.4 = (f32[1024,768]{1,0:T(8,128)S(1)}, f32[1024,768]{1,0:T(8,128)}, u32[]{:S(2)}) copy-start(f32[1024,768]{1,0:T(8,128)} %copy-done.3) | copy-start | bytes 9437188
  483.6 3.1 copy-start.9
  483.9 2.8 copy-start.59
  489.3 4.1 copy-start.28
  493.4 7.3 copy-start.23
  493.4 7.4 copy-start.25
  493.4 16.3 %slice-start = ((s8[12582912]{0:T(1024)(128)(4,1)}), s8[4194304]{0:T(1024)(128)(4,1)S(1)}, s32[]{:S(2)}) async-start(s8[12582912]{0:T(1024)(128)(4,1)} %bitcast.136), calls=%async_computation.10 | async-start | bytes 8388608
  493.4 16.3 %slice-start.1 = ((s8[12582912]{0:T(1024)(128)(4,1)}), s8[4194304]{0:T(1024)(128)(4,1)S(1)}, s32[]{:S(2)}) async-start(s8[12582912]{0:T(1024)(128)(4,1)} %bitcast.136), calls=%async_computation.11 | async-start | bytes 8388608
  500.8 8.9 slice-start.2
  509.7 6.9 copy-start.6
  516.7 2.0 copy-start.7
  530.5 2.9 copy-start.58
  535.1 1.9 copy-start.10
  535.1 2.2 copy-start.26
  541.7 24.1 %all-to-all-start.1 = ((bf16[32,13,768]{2,1,0:T(8,128)(2,1)}), bf16[32,13,768]{2,1,0:T(8,128)(2,1)}, u32[]{:S(2)}, u32[]{:S(2)}) async-start(bf16[32,13,768]{2,1,0:T(8,128)(2,1)} %all_to_all.17), calls=%async_computation.1 | async-start | bytes 1572864 | tf_op jit(solution)/shard_map/all_to_all | solution.py:242
  545.2 20.6 %copy-start.31 = (f32[768]{0:T(1024)S(1)}, f32[768]{0:T(1024)}, u32[]{:S(2)}) copy-start(f32[768]{0:T(1024)} %param.42) | copy-start | bytes 9220
  545.3 24.5 %copy-start.33 = (f32[416]{0:T(512)S(1)}, f32[416]{0:T(512)}, u32[]{:S(2)}) copy-start(f32[416]{0:T(512)} %copy-done.32) | copy-start | bytes 4996
  545.3 24.5 %copy-start.37 = (f32[416]{0:T(512)S(1)}, f32[416]{0:T(512)}, u32[]{:S(2)}) copy-start(f32[416]{0:T(512)} %copy-done.36) | copy-start | bytes 4996
  545.3 559.6 %all-reduce.4.cloned.1.call-start = ((), (), s32[]{:S(2)}) async-start(), calls=%async_computation.9 | async-start | bytes 69206016 | tf_op jit(solution)/shard_map/psum | solution.py:277
  556.3 13.5 %copy-start.2 = (f32[416,768]{1,0:T(8,128)S(1)}, f32[416,768]{1,0:T(8,128)}, u32[]{:S(2)}) copy-start(f32[416,768]{1,0:T(8,128)} %copy-done.1) | copy-start | bytes 3833860
  569.8 1.9 copy-start.11
  577.6 44.8 %copy-start.39 = (bf16[4,768]{1,0:T(4,128)(2,1)S(1)}, bf16[4,768]{1,0:T(4,128)(2,1)}, u32[]{:S(2)}) copy-start(bf16[4,768]{1,0:T(4,128)(2,1)} %param.40) | copy-start | bytes 18436
  1111.4 3.4 copy-start.18
  1114.8 2.5 copy-start.17
  1117.3 2.5 copy-start.16
  1119.8 10.7 slice-start.3
  1121.2 9.3 slice-start.4
  1121.2 9.3 slice-start.5
  (19 other events, 23.1 us)
Sparse Core Ops, SparseCore 0:
  10.9 61.6 all-gather.7
  75.5 55.1 all-gather.13
  133.6 52.9 all-gather.11
  189.3 52.9 all-gather.9
  245.1 52.9 all-gather.15
  300.8 62.5 all-gather.17
  366.3 62.4 all-gather.19
  577.7 527.0 all-reduce.3
where the time goes:
time: 1150 us; the launch traced here: 1140 us
  waiting for transfers between devices  788 us (69%)
  matrix products  173 us (15%)
  local copies, waits for them, and re-layouts  74.1 us (6%)
  blocking collectives  43.5 us (4%)
  other arithmetic  39.3 us (3%)
  between operations  16 us (1%)
    psum x1, waiting for transfers between devices, body(): lax.psum((grad_w_img, grad_w_box, grad_b_img, grad_g_reg, grad_beta_reg,...  477 us
    all_gather x1, waiting for transfers between devices, body(): lax.all_gather(w_img, ('enc', 'dp'), axis=0, tiled=True)  61.4 us
    all_gather x1, waiting for transfers between devices, body(): lax.all_gather(w_up, ('enc', 'dp'), axis=0, tiled=True)  59.7 us
    all_gather x1, waiting for transfers between devices, body(): lax.all_gather(w_value, ('enc', 'dp'), axis=0, tiled=True)  48.1 us
    all_gather x1, waiting for transfers between devices, body(): lax.all_gather(w_query, ('enc', 'dp'), axis=0, tiled=True)  48 us
    psum x1, blocking collectives, body(): lax.psum((grad_w_img, grad_w_box, grad_b_img, grad_g_reg, grad_beta_reg,...  43.5 us
    unnamed x158, local copies, waits for them, and re-layouts  43 us
    dot_general x7, matrix products, back_product(): jnp.einsum('rb,ab->ra', row_grad, weight, preferred_element_type=jnp.floa...  41 us
  transfers between devices with their start and end apart: 10, of which 10 were waited for; matrix products, arithmetic and copies ran while one was open for 11% of the time, Pallas kernels for 0%

commit v1 on v0

--- a/solution.py
+++ b/solution.py
@@ -275,29 +275,32 @@
         grad_g_two,
         grad_beta_two,
     ) = lax.psum(
-        (
-            grad_w_img,
-            grad_w_box,
-            grad_b_img,
-            grad_g_reg,
-            grad_beta_reg,
-            grad_w_query,
-            grad_b_query,
-            grad_w_key,
-            grad_w_value,
-            grad_b_value,
-            grad_w_out,
-            grad_b_out,
-            grad_g_one,
-            grad_beta_one,
-            grad_w_up,
-            grad_b_up,
-            grad_w_down,
-            grad_b_down,
-            grad_g_two,
-            grad_beta_two,
+        lax.psum(
+            (
+                grad_w_img,
+                grad_w_box,
+                grad_b_img,
+                grad_g_reg,
+                grad_beta_reg,
+                grad_w_query,
+                grad_b_query,
+                grad_w_key,
+                grad_w_value,
+                grad_b_value,
+                grad_w_out,
+                grad_b_out,
+                grad_g_one,
+                grad_beta_one,
+                grad_w_up,
+                grad_b_up,
+                grad_w_down,
+                grad_b_down,
+                grad_g_two,
+                grad_beta_two,
+            ),
+            "dp",
         ),
-        ("enc", "dp"),
+        "enc",
     )
     return (
         output,

time: 1150 us -> 2190 us (1.90)
  waiting for transfers between devices: 788 us -> 1820 us
    psum x0 -> x1, waiting for transfers between devices: none -> 1090 us  [body(): lax.psum(lax.psum((grad_w_img, grad_w_box, grad_b_img, grad_g_reg, grad_b...]
    psum x1, waiting for transfers between devices: 477 us -> 414 us  [body(): lax.psum((grad_w_img, grad_w_box, grad_b_img, grad_g_reg, grad_beta_reg,...]
    psum x0 -> x1, blocking collectives: none -> 30.9 us  [body(): lax.psum(lax.psum((grad_w_img, grad_w_box, grad_b_img, grad_g_reg, grad_b...]
  transfers between devices with their start and end apart: 10 -> 11, of which waited for: 10 -> 11; matrix products, arithmetic and copies ran while one was open for 11% -> 6% of each run, Pallas kernels for 0% -> 0%
where the time goes in v1:
time: 2190 us; the launch traced here: 2180 us
  waiting for transfers between devices  1820 us (83%)
  matrix products  172 us (8%)
  local copies, waits for them, and re-layouts  74.1 us (3%)
  blocking collectives  55.7 us (3%)
  other arithmetic  39.3 us (2%)
    psum x1, waiting for transfers between devices, body(): lax.psum(lax.psum((grad_w_img, grad_w_box, grad_b_img, grad_g_reg, grad_b...  1090 us
    psum x1, waiting for transfers between devices, body(): lax.psum((grad_w_img, grad_w_box, grad_b_img, grad_g_reg, grad_beta_reg,...  414 us
    all_gather x1, waiting for transfers between devices, body(): lax.all_gather(w_img, ('enc', 'dp'), axis=0, tiled=True)  61.4 us
    all_gather x1, waiting for transfers between devices, body(): lax.all_gather(w_up, ('enc', 'dp'), axis=0, tiled=True)  59.7 us
    all_gather x1, waiting for transfers between devices, body(): lax.all_gather(w_value, ('enc', 'dp'), axis=0, tiled=True)  48.1 us
    all_gather x1, waiting for transfers between devices, body(): lax.all_gather(w_query, ('enc', 'dp'), axis=0, tiled=True)  48 us
  transfers between devices with their start and end apart: 11, of which 11 were waited for; matrix products, arithmetic and copies ran while one was open for 6% of the time, Pallas kernels for 0%

profile of v1, /device:TPU:0, one launch (start us, length us, event | category | flops | bytes accessed | tf_op | source)
XLA Modules:
  0.0 2183.6 jit_solution(10767650444943801594)
XLA Ops:
  11.2 61.4 %all-gather.8.cloned.1.call-done = bf16[2048,768]{1,0:T(8,128)(2,1)} async-done(((bf16[64,768]{1,0:T(8,128)(2,1)}), bf16[2048,768]{1,0:T(8,128)(2,1)}) %all-gather.8.cloned.1.call-update) | async-done | bytes 3145744 | tf_op jit(solution)/shard_map/all_gather | solution.py:73
  72.6 3.4 fusion.82
  79.5 3.4 all-to-all-start
  85.8 2.6 select_compare_fusion
  89.0 2.6 select_add_fusion
  91.7 12.7 all-to-all-done
  106.5 24.1 %all-gather.14.cloned.1.call-done = bf16[768,768]{1,0:T(8,128)(2,1)} async-done(((bf16[24,768]{1,0:T(8,128)(2,1)}), bf16[768,768]{1,0:T(8,128)(2,1)}) %all-gather.14.cloned.1.call-update) | async-done | bytes 1179664 | tf_op jit(solution)/shard_map/all_gather | solution.py:75
  130.7 3.8 convolution_convert_fusion.2
  134.5 1.7 copy.66
  136.2 2.4 reshape.314
  138.6 48.0 %all-gather.12.cloned.1.call-done = bf16[768,768]{1,0:T(8,128)(2,1)} async-done(((bf16[24,768]{1,0:T(8,128)(2,1)}), bf16[768,768]{1,0:T(8,128)(2,1)}) %all-gather.12.cloned.1.call-update) | async-done | bytes 1179664 | tf_op jit(solution)/shard_map/all_gather | solution.py:74
  186.6 3.1 add_convert_fusion.3
  189.7 1.6 copy.65
  191.4 2.9 reshape.313
  194.3 48.1 %all-gather.10.cloned.1.call-done = bf16[768,768]{1,0:T(8,128)(2,1)} async-done(((bf16[24,768]{1,0:T(8,128)(2,1)}), bf16[768,768]{1,0:T(8,128)(2,1)}) %all-gather.10.cloned.1.call-update) | async-done | bytes 1179664 | tf_op jit(solution)/shard_map/all_gather | solution.py:76
  242.3 4.3 add_convert_fusion.4
  246.6 2.6 copy.64
  249.2 3.9 reshape.312
  253.0 7.8 fusion.39
  260.8 12.9 fusion.78
  274.9 3.4 copy-done.8
  279.7 1.5 copy.89
  281.2 16.9 all-gather.16.cloned.1.call-done
  298.1 3.4 fusion.79
  301.6 1.6 copy-done.3
  303.7 59.7 %all-gather.18.cloned.1.call-done = bf16[768,3072]{1,0:T(8,128)(2,1)} async-done(((bf16[24,3072]{1,0:T(8,128)(2,1)}), bf16[768,3072]{1,0:T(8,128)(2,1)}) %all-gather.18.cloned.1.call-update) | async-done | bytes 4718608 | tf_op jit(solution)/shard_map/all_gather | solution.py:78
  363.4 38.1 %multiply_convert_fusion.1 = (bf16[1024,3072]{1,0:T(8,128)(2,1)}, f32[1024,3072]{1,0:T(8,128)}, f32[1024,3072]{1,0:T(8,128)}) fusion(f32[3072]{0:T(1024)S(1)} %copy-done.60, bf16[768,3072]{1,0:T(8,128)(2,1)} %all-gather.18.cloned.1.call-done, f32[1024,768]{1,0:T(8,128)} %copy-done.3, f32[768]{0:T(1024)S(1)} %copy-done.34, f32[768]{0:T(1024)S(1)} %copy-done.29, ...), kind=kOutput, calls=%fused_computation.7 | convolution fusion | flops 5043388416 | bytes 39348224 | tf_op jit(solution)/shard_map/dot_general | solution.py:165
  401.5 27.3 %all-gather.20.cloned.1.call-done = bf16[3072,768]{1,0:T(8,128)(2,1)} async-done(((bf16[96,768]{1,0:T(8,128)(2,1)}), bf16[3072,768]{1,0:T(8,128)(2,1)}) %all-gather.20.cloned.1.call-update) | async-done | bytes 4718608 | tf_op jit(solution)/shard_map/all_gather | solution.py:79
  428.8 9.3 fusion.80
  439.6 2.4 multiply_reduce_fusion.1
  442.0 3.7 convert_reduce_fusion.1
  445.8 7.8 fusion.68
  453.6 18.8 convert_reduce_fusion
  472.4 10.1 multiply_reduce_fusion.2
  483.9 2.8 fusion.65
  486.7 2.6 convolution_convert_fusion.1
  489.3 1.7 copy.72
  491.1 2.4 reshape.315
  493.4 7.3 convert_reduce_fusion.3
  500.8 8.9 multiply_reduce_fusion
  509.7 6.9 multiply_convert_fusion
  516.7 2.0 fusion.31
  521.6 2.9 fusion.87
  527.6 2.9 fusion.85
  530.5 2.9 fusion.86
  533.4 1.7 fusion.83
  535.1 1.5 fusion.84
  537.3 1.6 add_convert_fusion.1
  541.7 3.5 all-to-all-start.1
  545.3 11.0 fusion.81
  556.3 9.5 all-to-all-done.1
  565.9 1.5 convert_reduce_fusion.6
  567.5 2.3 reshape.319
  569.8 1.9 multiply_reduce_fusion.9
  573.0 4.5 convolution_bitcast_fusion
  577.6 414.3 %all-reduce.7.cloned.1.call-done = (f32[2048,768]{0,1:T(8,128)}, f32[768,768]{1,0:T(8,128)}, f32[768,768]{1,0:T(8,128)}, f32[768,768]{1,0:T(8,128)}, f32[768,768...) async-done(((f32[2048,768]{0,1:T(8,128)}, f32[768,768]{1,0:T(8,128)}, f32[768,768]{1,0:T(8,128)}, f32[768,768]{1,0:T(8,128)}, f32[768,768]{1,0:T(8,128)}, ...) | async-done | bytes 34603024 | tf_op jit(solution)/shard_map/psum | solution.py:278
  993.2 24.8 %all-reduce = (f32[4,768]{1,0:T(4,128)S(1)}, f32[768]{0:T(1024)S(1)}, f32[768]{0:T(1024)S(1)}, f32[768]{0:T(1024)S(1)}, f32[768]{0:T(1024)S(1)}, /*index=5*/f32[...) all-reduce(f32[4,768]{1,0:T(4,128)S(1)} %convolution_bitcast_fusion, ...), channel_id=1, replica_groups=mesh['enc'=4,'dp'=8] {'dp'}, use_global_device_ids=true, to_apply=%region_18.20 | all-reduce | flops 14592 | bytes 116736 | tf_op jit(solution)/shard_map/psum | solution.py:278
  1018.1 30.9 %all-reduce.2 = (f32[4,768]{1,0:T(4,128)}, f32[768]{0:T(1024)}, f32[768]{0:T(1024)}, f32[768]{0:T(1024)}, f32[768]{0:T(1024)}, /*index=5*/f32[768]{0:T(1024)}, f...) all-reduce(f32[4,768]{1,0:T(4,128)S(1)} %get-tuple-element.105, ...), channel_id=1, replica_groups=mesh['enc'=4,'dp'=8] {'enc'}, use_global_device_ids=true, to_apply=%region_19.21 | all-reduce | flops 14592 | bytes 116736 | tf_op jit(solution)/shard_map/psum | solution.py:277
  1049.8 4.6 convolution_convert_fusion
  1054.5 1092.9 %all-reduce.9.cloned.1.call-done = (f32[2048,768]{0,1:T(8,128)}, f32[768,768]{1,0:T(8,128)}, f32[768,768]{1,0:T(8,128)}, f32[768,768]{1,0:T(8,128)}, f32[768,768...) async-done(((f32[2048,768]{0,1:T(8,128)}, f32[768,768]{1,0:T(8,128)}, f32[768,768]{1,0:T(8,128)}, f32[768,768]{1,0:T(8,128)}, f32[768,768]{1,0:T(8,128)}, ...) | async-done | bytes 34603024 | tf_op jit(solution)/shard_map/psum | solution.py:277
  2147.4 6.6 copy.84
  2153.9 3.4 copy.133
  2163.7 9.3 copy.137
  2173.1 3.7 copy.138
  (216 shorter events, 38.0 us)
Async XLA Ops:
  7.2 65.4 %copy-start = (bf16[416,2048]{1,0:T(8,128)(2,1)S(1)}, bf16[416,2048]{1,0:T(8,128)(2,1)}, u32[]{:S(2)}) copy-start(bf16[416,2048]{1,0:T(8,128)(2,1)} %param.34) | copy-start | bytes 5111812
  7.2 65.4 %all-gather.8.cloned.1.call-start = ((), (), s32[]{:S(2)}) async-start(), calls=%async_computation.2 | async-start | bytes 3244032 | tf_op jit(solution)/shard_map/all_gather | solution.py:73
  7.9 122.7 %all-gather.14.cloned.1.call-start = ((), (), s32[]{:S(2)}) async-start(), calls=%async_computation.5 | async-start | bytes 1216512 | tf_op jit(solution)/shard_map/all_gather | solution.py:75
  8.7 177.9 %all-gather.12.cloned.1.call-start = ((), (), s32[]{:S(2)}) async-start(), calls=%async_computation.4 | async-start | bytes 1216512 | tf_op jit(solution)/shard_map/all_gather | solution.py:74
  9.4 232.9 %all-gather.10.cloned.1.call-start = ((), (), s32[]{:S(2)}) async-start(), calls=%async_computation.3 | async-start | bytes 1216512 | tf_op jit(solution)/shard_map/all_gather | solution.py:76
  10.0 288.1 %all-gather.16.cloned.1.call-start = ((), (), s32[]{:S(2)}) async-start(), calls=%async_computation.6 | async-start | bytes 1216512 | tf_op jit(solution)/shard_map/all_gather | solution.py:77
  10.6 352.9 %all-gather.18.cloned.1.call-start = ((), (), s32[]{:S(2)}) async-start(), calls=%async_computation.7 | async-start | bytes 4866048 | tf_op jit(solution)/shard_map/all_gather | solution.py:78
  11.2 64.8 %copy-start.38 = (bf16[4,768]{1,0:T(4,128)(2,1)S(1)}, bf16[4,768]{1,0:T(4,128)(2,1)}, u32[]{:S(2)}) copy-start(bf16[4,768]{1,0:T(4,128)(2,1)} %param.40) | copy-start | bytes 18436
  11.2 64.8 %copy-start.41 = (bf16[4,416]{1,0:T(4,128)(2,1)S(1)}, bf16[4,416]{1,0:T(4,128)(2,1)}, u32[]{:S(2)}) copy-start(bf16[4,416]{1,0:T(4,128)(2,1)} %param.35) | copy-start | bytes 9988
  11.2 64.8 %copy-start.47 = (f32[768]{0:T(1024)S(1)}, f32[768]{0:T(1024)}, u32[]{:S(2)}) copy-start(f32[768]{0:T(1024)} %param.41) | copy-start | bytes 9220
  76.0 2.1 copy-start.30
  76.0 2.1 copy-start.48
  76.5 7.8 copy-start.46
  76.5 7.8 copy-start.56
  79.5 24.9 %all-to-all-start = ((bf16[32,13,768]{2,1,0:T(8,128)(2,1)}), bf16[32,13,768]{2,1,0:T(8,128)(2,1)S(1)}, u32[]{:S(2)}, u32[]{:S(2)}) async-start(bf16[32,13,768]{2,1,0:T(8,128)(2,1)} %all_to_all.14), calls=%async_computation | async-start | bytes 1572864 | tf_op jit(solution)/shard_map/all_to_all | solution.py:97
  82.9 345.9 %all-gather.20.cloned.1.call-start = ((), (), s32[]{:S(2)}) async-start(), calls=%async_computation.8 | async-start | bytes 4866048 | tf_op jit(solution)/shard_map/all_gather | solution.py:79
  88.4 16.9 copy-start.54
  88.4 16.8 copy-start.50
  91.6 13.6 copy-start.52
  106.5 24.1 %copy-start.19 = (bf16[4,256,768]{2,1,0:T(8,128)(2,1)}, bf16[4,256,768]{2,1,0:T(8,128)(2,1)S(1)}, u32[]{:S(2)}) copy-start(bf16[4,256,768]{2,1,0:T(8,128)(2,1)S(1)} %pad_maximum_fusion) | copy-start | bytes 4718596
  134.5 52.1 %copy-start.61 = (f32[768]{0:T(1024)S(1)}, f32[768]{0:T(1024)}, u32[]{:S(2)}) copy-start(f32[768]{0:T(1024)} %param.45) | copy-start | bytes 9220
  189.7 52.6 %copy-start.62 = (f32[768]{0:T(1024)S(1)}, f32[768]{0:T(1024)}, u32[]{:S(2)}) copy-start(f32[768]{0:T(1024)} %param.48) | copy-start | bytes 9220
  194.2 58.8 %copy-start.5 = (bf16[4,256,12,64]{1,0,3,2:T(4,128)(2,1)}, bf16[4,256,12,64]{1,0,3,2:T(4,128)(2,1)S(1)}, u32[]{:S(2)}) copy-start(bf16[4,256,12,64]{1,0,3,2:T(4,128)(2,1)S(1)} %reshape.313) | copy-start | bytes 4718596
  260.8 12.9 copy-start.22
  273.7 4.5 copy-start.8
  273.7 4.8 copy-start.27
  278.5 19.6 copy-start.20
  278.5 19.6 copy-start.63
  301.5 61.9 %copy-start.29 = (f32[768]{0:T(1024)S(1)}, f32[768]{0:T(1024)}, u32[]{:S(2)}) copy-start(f32[768]{0:T(1024)} %param.51) | copy-start | bytes 9220
  301.5 61.9 %copy-start.34 = (f32[768]{0:T(1024)S(1)}, f32[768]{0:T(1024)}, u32[]{:S(2)}) copy-start(f32[768]{0:T(1024)} %param.52) | copy-start | bytes 9220
  301.5 61.9 %copy-start.60 = (f32[3072]{0:T(1024)S(1)}, f32[3072]{0:T(1024)}, u32[]{:S(2)}) copy-start(f32[3072]{0:T(1024)} %param.54) | copy-start | bytes 36868
  303.7 125.1 %copy-start.64 = (f32[768]{0:T(1024)S(1)}, f32[768]{0:T(1024)}, u32[]{:S(2)}) copy-start(f32[768]{0:T(1024)} %param.56) | copy-start | bytes 9220
  438.7 3.3 copy-start.49
  439.6 6.2 slice-start.6
  442.0 3.7 slice-start.7
  445.8 7.8 copy-start.15
  453.6 18.8 copy-start.4
  483.6 3.1 copy-start.9
  483.9 2.8 copy-start.59
  489.3 4.1 copy-start.28
  493.4 7.3 copy-start.23
  493.4 7.4 copy-start.25
  493.4 16.3 slice-start
  493.4 16.3 slice-start.1
  500.8 8.9 slice-start.2
  509.7 6.9 copy-start.6
  516.7 2.0 copy-start.7
  530.5 2.9 copy-start.58
  535.1 2.2 copy-start.26
  541.7 24.1 %all-to-all-start.1 = ((bf16[32,13,768]{2,1,0:T(8,128)(2,1)}), bf16[32,13,768]{2,1,0:T(8,128)(2,1)}, u32[]{:S(2)}, u32[]{:S(2)}) async-start(bf16[32,13,768]{2,1,0:T(8,128)(2,1)} %all_to_all.17), calls=%async_computation.1 | async-start | bytes 1572864 | tf_op jit(solution)/shard_map/all_to_all | solution.py:242
  545.2 20.6 copy-start.31
  545.3 24.5 %copy-start.33 = (f32[416]{0:T(512)S(1)}, f32[416]{0:T(512)}, u32[]{:S(2)}) copy-start(f32[416]{0:T(512)} %copy-done.32) | copy-start | bytes 4996
  545.3 24.5 %copy-start.37 = (f32[416]{0:T(512)S(1)}, f32[416]{0:T(512)}, u32[]{:S(2)}) copy-start(f32[416]{0:T(512)} %copy-done.36) | copy-start | bytes 4996
  545.3 446.6 %all-reduce.7.cloned.1.call-start = ((), (), s32[]{:S(2)}) async-start(), calls=%async_computation.9 | async-start | bytes 69206016 | tf_op jit(solution)/shard_map/psum | solution.py:278
  556.3 13.5 copy-start.2
  569.8 1.9 copy-start.11
  577.6 1569.8 %all-reduce.9.cloned.1.call-start = ((), (), s32[]{:S(2)}) async-start(), calls=%async_computation.10 | async-start | bytes 69206016 | tf_op jit(solution)/shard_map/psum | solution.py:277
  991.9 57.0 %copy-start.39 = (bf16[4,768]{1,0:T(4,128)(2,1)S(1)}, bf16[4,768]{1,0:T(4,128)(2,1)}, u32[]{:S(2)}) copy-start(bf16[4,768]{1,0:T(4,128)(2,1)} %param.40) | copy-start | bytes 18436
  2153.9 3.4 copy-start.18
  2157.3 2.5 copy-start.17
  2159.8 2.5 copy-start.16
  2162.3 10.7 slice-start.3
  2163.7 9.3 slice-start.4
  2163.7 9.3 slice-start.5
  (20 other events, 25.0 us)
Sparse Core Ops, SparseCore 0:
  10.9 61.6 all-gather.7
  75.5 55.1 all-gather.13
  133.6 52.9 all-gather.11
  189.3 52.9 all-gather.9
  245.1 52.9 all-gather.15
  300.8 62.5 all-gather.17
  366.3 62.4 all-gather.19
  577.7 414.1 all-reduce.6
  995.3 1151.9 all-reduce.8
